TPU v7x, 32 devices: a whole 2x2x4 slice. The times are simulated.
32 devices in a mesh: expert: 8 (over z, x), pair: 2 (over core), dp: 2 (over y).
Axes of the slice: x: 2, y: 2, z: 4, core: 2. Of those that a mesh axis runs over, the one named last changes fastest.
Arguments:
- tokens: bfloat16 [128, 196, 768], P(('expert', 'pair', 'dp')), may hold values from -96 to 96
- phi: bfloat16 [768, 16], replicated, may hold values from -0.25 to 0.25
- w_in: bfloat16 [8, 768, 3072], P('expert', None, 'pair'), may hold values from -0.21875 to 0.21875
- w_out: bfloat16 [8, 3072, 768], P('expert', 'pair'), may hold values from -0.109375 to 0.109375
- slot_out: bfloat16 [128, 16, 768], P(('expert', 'pair', 'dp')), may hold values from -6 to 6
- grad_out: bfloat16 [128, 196, 768], P(('expert', 'pair', 'dp')), may hold values from -6 to 6
Outputs:
- token_grad: bfloat16 [128, 196, 768], P(('expert', 'pair', 'dp'))
- phi_grad: float32 [768, 16], replicated
- grad_w_in: bfloat16 [8, 768, 3072], P('expert', 'dp', 'pair')
- grad_w_out: bfloat16 [8, 3072, 768], P('expert', 'pair', 'dp')
All inputs are finite; a program needn't handle non-finite values.
Results may differ from a plain program's by a relative error of at most 0.0086.
Values may be sent and summed in bfloat16 or wider, within the bound.
A program may use at most 128 MiB of HBM per device.

v0:
```python
import jax
import jax.numpy as jnp
from jax import lax
from jax.sharding import PartitionSpec as P


def expert_rows(z_rows, g_rows, w_first, w_second):
    pre = jnp.dot(z_rows, w_first, preferred_element_type=jnp.float32)
    act_full, gelu_back = jax.vjp(jax.nn.gelu, pre)
    act = act_full.astype(jnp.bfloat16)
    dact = lax.dot_general(
        g_rows, w_second, (((1,), (1,)), ((), ())), preferred_element_type=jnp.float32
    )
    dpre = gelu_back(dact)[0].astype(jnp.bfloat16)
    grad_second = lax.dot_general(
        act, g_rows, (((0,), (0,)), ((), ())), preferred_element_type=jnp.float32
    )
    grad_first = lax.dot_general(
        z_rows, dpre, (((0,), (0,)), ((), ())), preferred_element_type=jnp.float32
    )
    back = lax.dot_general(
        dpre, w_first, (((1,), (1,)), ((), ())), preferred_element_type=jnp.float32
    )
    return (grad_first, grad_second, back)


def local(tokens, phi, w_in, w_out, slot_out, grad_out):
    f32 = jnp.float32
    images, _, width = tokens.shape
    groups = lax.axis_size("expert")
    per_group = phi.shape[1] // groups
    experts_here = w_in.shape[0]
    slots = per_group // experts_here
    logits = jnp.einsum("bmd,ds->bms", tokens, phi, preferred_element_type=f32)
    dispatch = jax.nn.softmax(logits, axis=1)
    combine = jax.nn.softmax(logits, axis=2)
    dispatch_low = dispatch.astype(jnp.bfloat16)
    combine_low = combine.astype(jnp.bfloat16)
    slot_in = jnp.einsum("bms,bmd->bsd", dispatch_low, tokens, preferred_element_type=f32).astype(
        jnp.bfloat16
    )
    slot_grad = jnp.einsum(
        "bms,bmd->bsd", combine_low, grad_out, preferred_element_type=f32
    ).astype(jnp.bfloat16)
    outgoing_in = slot_in.reshape(images, groups, per_group, width)
    outgoing_grad = slot_grad.reshape(images, groups, per_group, width)
    arrived_in, arrived_grad = (
        lax.all_to_all(outgoing_in, "expert", split_axis=1, concat_axis=0, tiled=True),
        lax.all_to_all(outgoing_grad, "expert", split_axis=1, concat_axis=0, tiled=True),
    )
    rows_in, rows_grad = (
        lax.all_gather(arrived_in, "pair", axis=0, tiled=True),
        lax.all_gather(arrived_grad, "pair", axis=0, tiled=True),
    )
    count = rows_in.shape[0]
    z_rows = rows_in[:, 0].reshape(count * slots, width)
    g_rows = rows_grad[:, 0].reshape(count * slots, width)
    grad_first, grad_second, back = expert_rows(z_rows, g_rows, w_in[0], w_out[0])
    firsts = [grad_first]
    seconds = [grad_second]
    backs = back.reshape(count, 1, slots, width)
    back_sum = lax.psum_scatter(backs, "pair", scatter_dimension=0, tiled=True)
    grad_w_in = lax.psum_scatter(
        jnp.stack(firsts).astype(jnp.bfloat16), "dp", scatter_dimension=1, tiled=True
    )
    grad_w_out = lax.psum_scatter(
        jnp.stack(seconds).astype(jnp.bfloat16), "dp", scatter_dimension=2, tiled=True
    )
    back_low = back_sum.astype(jnp.bfloat16)
    returned = lax.all_to_all(back_low, "expert", split_axis=0, concat_axis=1, tiled=True)
    slot_in_grad = returned.reshape(images, groups * per_group, width)
    dispatch_grad = jnp.einsum("bmd,bsd->bms", tokens, slot_in_grad, preferred_element_type=f32)
    combine_grad = jnp.einsum("bmd,bsd->bms", grad_out, slot_out, preferred_element_type=f32)
    logit_grad = dispatch * (
        dispatch_grad - jnp.sum(dispatch * dispatch_grad, axis=1, keepdims=True)
    )
    logit_grad = logit_grad + combine * (
        combine_grad - jnp.sum(combine * combine_grad, axis=2, keepdims=True)
    )
    logit_low = logit_grad.astype(jnp.bfloat16)
    token_part = jnp.einsum("bms,bsd->bmd", dispatch_low, slot_in_grad, preferred_element_type=f32)
    token_grad = (
        token_part + jnp.einsum("bms,ds->bmd", logit_low, phi, preferred_element_type=f32)
    ).astype(jnp.bfloat16)
    phi_part = jnp.einsum("bmd,bms->ds", tokens, logit_low, preferred_element_type=f32)
    phi_grad = lax.psum(phi_part, ("expert", "pair", "dp"))
    return (token_grad, phi_grad, grad_w_in, grad_w_out)


def solution(mesh):
    in_specs = (
        P(("expert", "pair", "dp"), None, None),
        P(),
        P("expert", None, "pair"),
        P("expert", "pair", None),
        P(("expert", "pair", "dp"), None, None),
        P(("expert", "pair", "dp"), None, None),
    )
    out_specs = (
        P(("expert", "pair", "dp"), None, None),
        P(),
        P("expert", "dp", "pair"),
        P("expert", "pair", "dp"),
    )
    return jax.shard_map(local, mesh=mesh, in_specs=in_specs, out_specs=out_specs, check_vma=False)
```

profile of v0, /device:TPU:0, one launch (start us, length us, event | category | flops | bytes accessed | tf_op | source)
XLA Modules:
  0.0 153.0 jit_solution(3510893113097627227)
XLA Ops:
  7.2 1.8 %fusion.32 = f32[4,196,16]{1,2,0:T(8,128)S(1)} fusion(bf16[4,196,768]{2,0,1:T(4,128)(2,1)} %param.6, bf16[768,16]{0,1:T(8,128)(2,1)} %param.7), kind=kOutput, calls=%fused_computation.41 | convolution fusion | flops 19267584 | bytes 1278976 | tf_op jit(solution)/shard_map/bmd,ds->bms/dot_general | solution.py:34
  9.0 0.7 fusion.64
  9.7 1.6 %convolution_convert_fusion.3 = bf16[4,16,768]{2,1,0:T(8,128)(2,1)S(1)} fusion(bf16[4,196,768]{2,0,1:T(4,128)(2,1)} %param.11, f32[4,196]{1,0:T(4,128)S(1)} %get-tuple-element.16, f32[4,196,16]{1,2,0:T(8,128)S(1)} %fusion.32), kind=kOutput, calls=%fused_computation.19 | convolution fusion | flops 19355168 | bytes 1355840 | tf_op jit(solution)/shard_map/bms,bmd->bsd/dot_general | solution.py:42
  11.4 0.7 copy.32
  12.1 7.3 %all-to-all-start = ((bf16[4,8,2,768]{3,2,0,1:T(2,128)(2,1)}), bf16[4,8,2,768]{3,2,0,1:T(2,128)(2,1)S(1)}, u32[]{:S(2)}, u32[]{:S(2)}) async-start(bf16[4,8,2,768]{3,2,0,1:T(2,128)(2,1)} %copy.32), calls=%async_computation | async-start | bytes 196608 | tf_op jit(solution)/shard_map/all_to_all | solution.py:49
  19.3 0.7 fusion.65
  20.1 1.6 %convolution_convert_fusion.2 = bf16[4,16,768]{2,1,0:T(8,128)(2,1)S(1)} fusion(bf16[4,196,768]{2,0,1:T(4,128)(2,1)} %param.6, f32[4,16]{1,0:T(4,128)S(1)} %get-tuple-element.18, f32[4,196,16]{1,2,0:T(8,128)S(1)} %fusion.32), kind=kOutput, calls=%fused_computation.18 | convolution fusion | flops 19354628 | bytes 1352960 | tf_op jit(solution)/shard_map/bms,bmd->bsd/dot_general | solution.py:39
  21.7 0.7 copy.35
  22.4 4.0 %all-to-all-done = bf16[4,8,2,768]{3,2,0,1:T(2,128)(2,1)S(1)} async-done(((bf16[4,8,2,768]{3,2,0,1:T(2,128)(2,1)}), bf16[4,8,2,768]{3,2,0,1:T(2,128)(2,1)S(1)}, u32[]{:S(2)}, u32[]{:S(2)}) %all-to-all-start) | async-done | bytes 98336 | tf_op jit(solution)/shard_map/all_to_all | solution.py:49
  26.5 3.4 %all-to-all-start.1 = ((bf16[4,8,2,768]{3,2,0,1:T(2,128)(2,1)}), bf16[4,8,2,768]{3,2,0,1:T(2,128)(2,1)S(1)}, u32[]{:S(2)}, u32[]{:S(2)}) async-start(bf16[4,8,2,768]{3,2,0,1:T(2,128)(2,1)} %copy.35), calls=%async_computation.1 | async-start | bytes 196608 | tf_op jit(solution)/shard_map/all_to_all | solution.py:48
  29.8 0.0 reduce-scatter.6.cloned.1.call-start
  29.9 1.9 %all_gather.6 = bf16[64,1,2,768]{3,2,1,0:T(2,128)(2,1)S(1)} all-gather(bf16[32,1,2,768]{3,2,1,0:T(2,128)(2,1)S(1)} %bitcast.73), channel_id=1, replica_groups=mesh['expert'=8,'pair'=2,'dp'=2] {'pair'}, dimensions={0}, use_global_device_ids=true | all-gather | bytes 294912 | tf_op jit(solution)/shard_map/all_gather | solution.py:53
  31.8 0.1 reshape_squeeze.6
  31.9 5.0 %all-to-all-done.1 = bf16[4,8,2,768]{3,2,0,1:T(2,128)(2,1)S(1)} async-done(((bf16[4,8,2,768]{3,2,0,1:T(2,128)(2,1)}), bf16[4,8,2,768]{3,2,0,1:T(2,128)(2,1)S(1)}, u32[]{:S(2)}, u32[]{:S(2)}) %all-to-all-start.1) | async-done | bytes 98336 | tf_op jit(solution)/shard_map/all_to_all | solution.py:48
  36.9 1.9 %all_gather.7 = bf16[64,1,2,768]{3,2,1,0:T(2,128)(2,1)S(1)} all-gather(bf16[32,1,2,768]{3,2,1,0:T(2,128)(2,1)S(1)} %bitcast.74), channel_id=1, replica_groups=mesh['expert'=8,'pair'=2,'dp'=2] {'pair'}, dimensions={0}, use_global_device_ids=true | all-gather | bytes 294912 | tf_op jit(solution)/shard_map/all_gather | solution.py:52
  38.8 0.1 reshape_squeeze.7
  38.9 0.5 fusion.8
  39.4 1.2 copy-done.7
  40.6 1.8 %fusion.40 = bf16[128,1536]{1,0:T(8,128)(2,1)} fusion(f32[128,1536]{1,0:T(8,128)S(1)} %fusion.8, bf16[128,768]{1,0:T(8,128)(2,1)S(1)} %reshape_squeeze.6, bf16[1,1536,768]{2,1,0:T(8,128)(2,1)S(1)} %copy-done.7), kind=kOutput, calls=%fused_computation.49 | convolution fusion | flops 305922048 | bytes 3735552 | tf_op jit(solution)/shard_map/dot_general | solution.py:11
  42.4 1.9 %reshape.35 = bf16[64,2,1536]{2,1,0:T(2,128)(2,1)} reshape(bf16[128,1536]{1,0:T(8,128)(2,1)} %fusion.40) | data formatting | bytes 786432 | tf_op jit(solution)/shard_map/reshape.16
  44.3 2.6 %fusion.12 = f32[64,1,2,768]{3,0,2,1:T(8,128)} fusion(bf16[1,768,1536]{2,1,0:T(8,128)(2,1)S(1)} %copy-done, bf16[64,2,1536]{2,1,0:T(2,128)(2,1)} %reshape.35), kind=kOutput, calls=%fused_computation.17 | convolution fusion | flops 301989888 | bytes 3145728 | tf_op jit(solution)/shard_map/dot_general | solution.py:21
  46.9 0.0 reduce-scatter.6.cloned.1.call-update
  46.9 0.0 reduce-scatter.10.cloned.1.call-start
  47.0 2.3 %fusion.5 = bf16[1,1536,768]{2,1,0:T(8,128)(2,1)} fusion(bf16[128,768]{1,0:T(8,128)(2,1)S(1)} %reshape_squeeze.6, f32[128,1536]{1,0:T(8,128)S(1)} %fusion.8), kind=kOutput, calls=%fused_computation.7 | convolution fusion | flops 304939008 | bytes 3342336 | tf_op jit(solution)/shard_map/dot_general | solution.py:15
  49.3 12.2 %copy.44 = bf16[1,1536,768]{1,0,2:T(2,128)(2,1)} copy(bf16[1,1536,768]{2,1,0:T(8,128)(2,1)} %fusion.5) | data formatting | bytes 4718592
  61.5 4.4 %copy.63 = bf16[768,1,1536]{2,0,1:T(8,128)(2,1)} copy(bf16[768,1,1536]{2,1,0:T(2,128)(2,1)} %bitcast.69) | data formatting | bytes 4718592
  65.8 0.0 reduce-scatter.10.cloned.1.call-update
  65.9 0.0 reduce-scatter.8.cloned.1.call-start
  65.9 0.9 copy-done.1
  66.8 2.2 %fusion.4 = bf16[1,768,1536]{2,1,0:T(8,128)(2,1)} fusion(bf16[128,768]{1,0:T(8,128)(2,1)S(1)} %reshape_squeeze.7, bf16[128,1536]{1,0:T(8,128)(2,1)S(1)} %copy-done.1), kind=kOutput, calls=%fused_computation.6 | convolution fusion | flops 303169536 | bytes 2949120 | tf_op jit(solution)/shard_map/dot_general | solution.py:18
  69.1 0.0 reduce-scatter.8.cloned.1.call-update
  69.1 0.9 copy-done.8
  70.0 1.8 %fusion.25 = f32[4,196,16]{1,2,0:T(8,128)S(1)} fusion(bf16[4,16,768]{2,1,0:T(8,128)(2,1)S(1)} %copy-done.8, bf16[4,196,768]{2,0,1:T(4,128)(2,1)} %param.11), kind=kOutput, calls=%fused_computation.34 | convolution fusion | flops 19267584 | bytes 1352704 | tf_op jit(solution)/shard_map/bmd,bsd->bms/dot_general | solution.py:73
  71.8 1.0 convert_element_type.44
  72.8 0.7 copy.38
  73.5 3.5 %all-to-all-start.2 = ((bf16[32,1,2,768]{3,2,1,0:T(2,128)(2,1)}), bf16[32,1,2,768]{3,2,1,0:T(2,128)(2,1)S(1)}, u32[]{:S(2)}, u32[]{:S(2)}) async-start(bf16[32,1,2,768]{3,2,1,0:T(2,128)(2,1)} %copy.38), calls=%async_computation.3 | async-start | bytes 196608 | tf_op jit(solution)/shard_map/all_to_all | solution.py:70
  77.1 0.2 fusion.23
  77.3 6.8 %all-to-all-done.2 = bf16[32,1,2,768]{3,2,1,0:T(2,128)(2,1)S(1)} async-done(((bf16[32,1,2,768]{3,2,1,0:T(2,128)(2,1)}), bf16[32,1,2,768]{3,2,1,0:T(2,128)(2,1)S(1)}, u32[]{:S(2)}, u32[]{:S(2)}) %all-to-all-start.2) | async-done | bytes 98336 | tf_op jit(solution)/shard_map/all_to_all | solution.py:70
  84.1 0.1 copy.64
  84.3 1.7 %convolution_bitcast_fusion = f32[4,196,16]{1,2,0:T(8,128)S(1)} fusion(bf16[4,16,768]{2,1,0:T(8,128)(2,1)S(1)} %reshape.36, bf16[4,196,768]{2,0,1:T(4,128)(2,1)} %param.6), kind=kOutput, calls=%fused_computation.24 | convolution fusion | flops 19267584 | bytes 1352704 | tf_op jit(solution)/shard_map/bmd,bsd->bms/dot_general | solution.py:72
  85.9 0.0 copy-start.3
  86.0 2.2 %fusion.28 = f32[4,196,768]{2,1,0:T(8,128)} fusion(f32[4,196,16]{1,2,0:T(8,128)S(1)} %fusion.23, f32[4,196,16]{1,2,0:T(8,128)S(1)} %convolution_bitcast_fusion, bf16[768,16]{0,1:T(8,128)(2,1)S(1)} %copy-done.6, f32[4,196,16]{1,2,0:T(8,128)S(1)} %copy-done.4, f32[4,16]{1,0:T(4,128)S(1)} %get-tuple-element.18), kind=kOutput, calls=%fused_computation.37 | convolution fusion | flops 19355652 | bytes 2583808 | tf_op jit(solution)/shard_map/bms,ds->bmd/dot_general | solution.py:83
  88.1 3.6 %add_convert_fusion = bf16[4,196,768]{2,1,0:T(8,128)(2,1)} fusion(f32[4,196,768]{2,1,0:T(8,128)} %fusion.28, bf16[4,16,768]{2,1,0:T(8,128)(2,1)S(1)} %reshape.36, f32[4,16]{1,0:T(4,128)S(1)} %get-tuple-element.18, f32[4,196,16]{1,2,0:T(8,128)S(1)} %copy-done.3), kind=kOutput, calls=%fused_computation.8 | convolution fusion | flops 20509700 | bytes 3761408 | tf_op jit(solution)/shard_map/bms,bsd->bmd/dot_general | solution.py:81
  91.7 2.8 %copy.43 = bf16[4,196,768]{2,0,1:T(4,128)(2,1)} copy(bf16[4,196,768]{2,1,0:T(8,128)(2,1)} %add_convert_fusion) | data formatting | bytes 2408448
  94.6 1.7 %convolution_bitcast_fusion.1 = f32[768,16]{0,1:T(8,128)S(1)} fusion(f32[4,196,16]{1,2,0:T(8,128)S(1)} %fusion.23, f32[4,196,16]{1,2,0:T(8,128)S(1)} %convolution_bitcast_fusion, bf16[4,196,768]{2,0,1:T(4,128)(2,1)} %param.6, f32[4,196,16]{1,2,0:T(8,128)S(1)} %copy-done.4, f32[4,16]{1,0:T(4,128)S(1)} %get-tuple-element.18), kind=kOutput, calls=%fused_computation.33 | convolution fusion | flops 19355652 | bytes 1404160 | tf_op jit(solution)/shard_map/bmd,bms->ds/dot_general | solution.py:85
  96.3 39.8 %psum.7 = f32[768,16]{0,1:T(8,128)} all-reduce(f32[768,16]{0,1:T(8,128)S(1)} %convolution_bitcast_fusion.1), channel_id=1, replica_groups=mesh['expert'=8,'pair'=2,'dp'=2] {'expert','pair','dp'}, use_global_device_ids=true, to_apply=%region_7.0 | all-reduce | flops 12288 | bytes 98304 | tf_op jit(solution)/shard_map/psum | solution.py:86
  136.1 3.9 %reshape_bitcast_fusion = bf16[1,1536,384]{1,0,2:T(2,128)(2,1)} fusion(bf16[384,1536]{1,0:T(8,128)(2,1)} %reduce-scatter.10.cloned.1.call-done), kind=kLoop, calls=%fused_computation.10 | loop fusion | bytes 2359296
  140.1 6.4 %copy.45 = bf16[1,1536,384]{2,1,0:T(8,128)(2,1)} copy(bf16[1,1536,384]{1,0,2:T(2,128)(2,1)} %reshape_bitcast_fusion) | data formatting | bytes 2359296
  (20 shorter events, 0.2 us)
Async XLA Ops:
  7.2 31.8 %copy-start = (bf16[1,768,1536]{2,1,0:T(8,128)(2,1)S(1)}, bf16[1,768,1536]{2,1,0:T(8,128)(2,1)}, u32[]{:S(2)}) copy-start(bf16[1,768,1536]{2,1,0:T(8,128)(2,1)} %param.8) | copy-start | bytes 7077892
  9.0 12.7 %copy-start.2 = (f32[4,196,16]{1,2,0:T(8,128)}, f32[4,196,16]{1,2,0:T(8,128)S(1)}, u32[]{:S(2)}) copy-start(f32[4,196,16]{1,2,0:T(8,128)S(1)} %fusion.32) | copy-start | bytes 150532
  12.1 14.4 %all-to-all-start = ((bf16[4,8,2,768]{3,2,0,1:T(2,128)(2,1)}), bf16[4,8,2,768]{3,2,0,1:T(2,128)(2,1)S(1)}, u32[]{:S(2)}, u32[]{:S(2)}) async-start(bf16[4,8,2,768]{3,2,0,1:T(2,128)(2,1)} %copy.32), calls=%async_computation | async-start | bytes 196608 | tf_op jit(solution)/shard_map/all_to_all | solution.py:49
  26.5 10.4 %all-to-all-start.1 = ((bf16[4,8,2,768]{3,2,0,1:T(2,128)(2,1)}), bf16[4,8,2,768]{3,2,0,1:T(2,128)(2,1)S(1)}, u32[]{:S(2)}, u32[]{:S(2)}) async-start(bf16[4,8,2,768]{3,2,0,1:T(2,128)(2,1)} %copy.35), calls=%async_computation.1 | async-start | bytes 196608 | tf_op jit(solution)/shard_map/all_to_all | solution.py:48
  29.8 42.0 %reduce-scatter.6.cloned.1.call-start = ((), (), s32[]{:S(2)}) async-start(), calls=%async_computation.6 | async-start | bytes 589824 | tf_op jit(solution)/shard_map/reduce_scatter | solution.py:62
  38.9 1.7 %copy-start.7 = (bf16[1,1536,768]{2,1,0:T(8,128)(2,1)S(1)}, bf16[1,1536,768]{2,1,0:T(8,128)(2,1)}, u32[]{:S(2)}) copy-start(bf16[1,1536,768]{2,1,0:T(8,128)(2,1)} %param.9) | copy-start | bytes 7077892
  46.9 89.2 %reduce-scatter.10.cloned.1.call-start = ((), (), s32[]{:S(2)}) async-start(), calls=%async_computation.8 | async-start | bytes 3538944
  65.8 1.0 copy-start.1
  65.9 80.6 %reduce-scatter.8.cloned.1.call-start = ((), (), s32[]{:S(2)}) async-start(), calls=%async_computation.7 | async-start | bytes 3538944 | tf_op jit(solution)/shard_map/reduce_scatter | solution.py:63
  69.1 0.9 copy-start.8
  70.0 7.1 %copy-start.5 = (f32[4,196,16]{1,2,0:T(8,128)S(1)}, f32[4,196,16]{1,2,0:T(8,128)}, u32[]{:S(2)}) copy-start(f32[4,196,16]{1,2,0:T(8,128)} %get-tuple-element.17) | copy-start | bytes 150532
  73.5 12.4 %copy-start.4 = (f32[4,196,16]{1,2,0:T(8,128)S(1)}, f32[4,196,16]{1,2,0:T(8,128)}, u32[]{:S(2)}) copy-start(f32[4,196,16]{1,2,0:T(8,128)} %get-tuple-element.19) | copy-start | bytes 150532
  73.5 12.4 %copy-start.6 = (bf16[768,16]{0,1:T(8,128)(2,1)S(1)}, bf16[768,16]{0,1:T(8,128)(2,1)}, u32[]{:S(2)}) copy-start(bf16[768,16]{0,1:T(8,128)(2,1)} %param.7) | copy-start | bytes 73732
  73.5 10.6 %all-to-all-start.2 = ((bf16[32,1,2,768]{3,2,1,0:T(2,128)(2,1)}), bf16[32,1,2,768]{3,2,1,0:T(2,128)(2,1)S(1)}, u32[]{:S(2)}, u32[]{:S(2)}) async-start(bf16[32,1,2,768]{3,2,1,0:T(2,128)(2,1)} %copy.38), calls=%async_computation.3 | async-start | bytes 196608 | tf_op jit(solution)/shard_map/all_to_all | solution.py:70
  85.9 2.2 %copy-start.3 = (f32[4,196,16]{1,2,0:T(8,128)S(1)}, f32[4,196,16]{1,2,0:T(8,128)}, u32[]{:S(2)}) copy-start(f32[4,196,16]{1,2,0:T(8,128)} %copy-done.2) | copy-start | bytes 150532
Sparse Core Ops, SparseCore 0:
  47.1 5.4 reduce-scatter.5
  66.0 32.4 reduce-scatter.9
  101.3 35.5 reduce-scatter.7
where the time goes:
time: 154 us; the launch traced here: 153 us
  blocking collectives  43.7 us (28%)
  local copies, waits for them, and re-layouts  37.2 us (24%)
  matrix products  25.5 us (17%)
  waiting for transfers between devices  15.9 us (10%)
  starting transfers between devices  14.3 us (9%)
  between operations  13.9 us (9%)
  other arithmetic  2.6 us (2%)
    psum x1, blocking collectives, local(): phi_grad = lax.psum(phi_part, ('expert', 'pair', 'dp'))  39.8 us
    unnamed x23, local copies, waits for them, and re-layouts  32.8 us
    all_to_all x1, starting transfers between devices, local(): lax.all_to_all(outgoing_grad, 'expert', split_axis=1, concat_axis=0, tile...  7.28 us
    all_to_all x1, waiting for transfers between devices, local(): lax.all_to_all(back_low, 'expert', split_axis=0, concat_axis=1, tiled=True)  6.84 us
    all_to_all x1, waiting for transfers between devices, local(): lax.all_to_all(outgoing_in, 'expert', split_axis=1, concat_axis=0, tiled=...  4.98 us
    all_to_all x1, waiting for transfers between devices, local(): lax.all_to_all(outgoing_grad, 'expert', split_axis=1, concat_axis=0, tile...  4.02 us
    dot_general x1, matrix products, local(): jnp.einsum('bms,bsd->bmd', dispatch_low, slot_in_grad, preferred_element_...  3.6 us
    all_to_all x1, starting transfers between devices, local(): lax.all_to_all(back_low, 'expert', split_axis=0, concat_axis=1, tiled=True)  3.49 us
  transfers between devices with their start and end apart: 6, of which 3 were waited for; matrix products, arithmetic and copies ran while one was open for 33% of the time, Pallas kernels for 0%

commit v1 on v0

--- a/solution.py
+++ b/solution.py
@@ -83,7 +83,7 @@
         token_part + jnp.einsum("bms,ds->bmd", logit_low, phi, preferred_element_type=f32)
     ).astype(jnp.bfloat16)
     phi_part = jnp.einsum("bmd,bms->ds", tokens, logit_low, preferred_element_type=f32)
-    phi_grad = lax.psum(phi_part, ("expert", "pair", "dp"))
+    phi_grad = lax.psum(lax.psum(phi_part, ("pair", "dp")), "expert")
     return (token_grad, phi_grad, grad_w_in, grad_w_out)
 
 

time: 154 us -> 163 us (1.058)
  blocking collectives: 43.7 us -> 52.2 us
    psum x1 -> x2, blocking collectives: 39.8 us -> 48.3 us  [local(): phi_grad = lax.psum(lax.psum(phi_part, ('pair', 'dp')), 'expert')]
  transfers between devices with their start and end apart: 6 -> 6, of which waited for: 3 -> 3; matrix products, arithmetic and copies ran while one was open for 33% -> 31% of each run, Pallas kernels for 0% -> 0%
where the time goes in v1:
time: 163 us; the launch traced here: 161 us
  blocking collectives  52.2 us (32%)
  local copies, waits for them, and re-layouts  37.1 us (23%)
  matrix products  25.5 us (16%)
  waiting for transfers between devices  15.9 us (10%)
  starting transfers between devices  14.3 us (9%)
  between operations  13.9 us (9%)
  other arithmetic  2.6 us (2%)
    psum x2, blocking collectives, local(): phi_grad = lax.psum(lax.psum(phi_part, ('pair', 'dp')), 'expert')  48.3 us
    unnamed x23, local copies, waits for them, and re-layouts  32.7 us
    all_to_all x1, starting transfers between devices, local(): lax.all_to_all(outgoing_grad, 'expert', split_axis=1, concat_axis=0, tile...  7.28 us
    all_to_all x1, waiting for transfers between devices, local(): lax.all_to_all(back_low, 'expert', split_axis=0, concat_axis=1, tiled=True)  6.84 us
    all_to_all x1, waiting for transfers between devices, local(): lax.all_to_all(outgoing_in, 'expert', split_axis=1, concat_axis=0, tiled=...  4.98 us
    all_to_all x1, waiting for transfers between devices, local(): lax.all_to_all(outgoing_grad, 'expert', split_axis=1, concat_axis=0, tile...  4.02 us
    dot_general x1, matrix products, local(): jnp.einsum('bms,bsd->bmd', dispatch_low, slot_in_grad, preferred_element_...  3.6 us
    all_to_all x1, starting transfers between devices, local(): lax.all_to_all(back_low, 'expert', split_axis=0, concat_axis=1, tiled=True)  3.49 us
  transfers between devices with their start and end apart: 6, of which 3 were waited for; matrix products, arithmetic and copies ran while one was open for 31% of the time, Pallas kernels for 0%

profile of v1, /device:TPU:0, one launch (start us, length us, event | category | flops | bytes accessed | tf_op | source)
XLA Modules:
  0.0 161.5 jit_solution(3264242103628984754)
XLA Ops:
  7.2 1.8 %fusion.32 = f32[4,196,16]{1,2,0:T(8,128)S(1)} fusion(bf16[4,196,768]{2,0,1:T(4,128)(2,1)} %param.6, bf16[768,16]{0,1:T(8,128)(2,1)} %param.7), kind=kOutput, calls=%fused_computation.41 | convolution fusion | flops 19267584 | bytes 1278976 | tf_op jit(solution)/shard_map/bmd,ds->bms/dot_general | solution.py:34
  9.0 0.7 fusion.64
  9.7 1.6 convolution_convert_fusion.3
  11.4 0.7 copy.32
  12.1 7.3 %all-to-all-start = ((bf16[4,8,2,768]{3,2,0,1:T(2,128)(2,1)}), bf16[4,8,2,768]{3,2,0,1:T(2,128)(2,1)S(1)}, u32[]{:S(2)}, u32[]{:S(2)}) async-start(bf16[4,8,2,768]{3,2,0,1:T(2,128)(2,1)} %copy.32), calls=%async_computation | async-start | bytes 196608 | tf_op jit(solution)/shard_map/all_to_all | solution.py:49
  19.3 0.7 fusion.65
  20.1 1.6 %convolution_convert_fusion.2 = bf16[4,16,768]{2,1,0:T(8,128)(2,1)S(1)} fusion(bf16[4,196,768]{2,0,1:T(4,128)(2,1)} %param.6, f32[4,16]{1,0:T(4,128)S(1)} %get-tuple-element.18, f32[4,196,16]{1,2,0:T(8,128)S(1)} %fusion.32), kind=kOutput, calls=%fused_computation.18 | convolution fusion | flops 19354628 | bytes 1352960 | tf_op jit(solution)/shard_map/bms,bmd->bsd/dot_general | solution.py:39
  21.7 0.7 copy.35
  22.4 4.0 %all-to-all-done = bf16[4,8,2,768]{3,2,0,1:T(2,128)(2,1)S(1)} async-done(((bf16[4,8,2,768]{3,2,0,1:T(2,128)(2,1)}), bf16[4,8,2,768]{3,2,0,1:T(2,128)(2,1)S(1)}, u32[]{:S(2)}, u32[]{:S(2)}) %all-to-all-start) | async-done | bytes 98336 | tf_op jit(solution)/shard_map/all_to_all | solution.py:49
  26.5 3.4 %all-to-all-start.1 = ((bf16[4,8,2,768]{3,2,0,1:T(2,128)(2,1)}), bf16[4,8,2,768]{3,2,0,1:T(2,128)(2,1)S(1)}, u32[]{:S(2)}, u32[]{:S(2)}) async-start(bf16[4,8,2,768]{3,2,0,1:T(2,128)(2,1)} %copy.35), calls=%async_computation.1 | async-start | bytes 196608 | tf_op jit(solution)/shard_map/all_to_all | solution.py:48
  29.8 0.0 reduce-scatter.6.cloned.1.call-start
  29.9 1.9 %all_gather.6 = bf16[64,1,2,768]{3,2,1,0:T(2,128)(2,1)S(1)} all-gather(bf16[32,1,2,768]{3,2,1,0:T(2,128)(2,1)S(1)} %bitcast.73), channel_id=1, replica_groups=mesh['expert'=8,'pair'=2,'dp'=2] {'pair'}, dimensions={0}, use_global_device_ids=true | all-gather | bytes 294912 | tf_op jit(solution)/shard_map/all_gather | solution.py:53
  31.8 0.1 reshape_squeeze.6
  31.9 5.0 %all-to-all-done.1 = bf16[4,8,2,768]{3,2,0,1:T(2,128)(2,1)S(1)} async-done(((bf16[4,8,2,768]{3,2,0,1:T(2,128)(2,1)}), bf16[4,8,2,768]{3,2,0,1:T(2,128)(2,1)S(1)}, u32[]{:S(2)}, u32[]{:S(2)}) %all-to-all-start.1) | async-done | bytes 98336 | tf_op jit(solution)/shard_map/all_to_all | solution.py:48
  36.9 1.9 %all_gather.7 = bf16[64,1,2,768]{3,2,1,0:T(2,128)(2,1)S(1)} all-gather(bf16[32,1,2,768]{3,2,1,0:T(2,128)(2,1)S(1)} %bitcast.74), channel_id=1, replica_groups=mesh['expert'=8,'pair'=2,'dp'=2] {'pair'}, dimensions={0}, use_global_device_ids=true | all-gather | bytes 294912 | tf_op jit(solution)/shard_map/all_gather | solution.py:52
  38.8 0.1 reshape_squeeze.7
  38.9 0.5 fusion.8
  39.4 1.2 copy-done.7
  40.6 1.8 %fusion.40 = bf16[128,1536]{1,0:T(8,128)(2,1)} fusion(f32[128,1536]{1,0:T(8,128)S(1)} %fusion.8, bf16[128,768]{1,0:T(8,128)(2,1)S(1)} %reshape_squeeze.6, bf16[1,1536,768]{2,1,0:T(8,128)(2,1)S(1)} %copy-done.7), kind=kOutput, calls=%fused_computation.49 | convolution fusion | flops 305922048 | bytes 3735552 | tf_op jit(solution)/shard_map/dot_general | solution.py:11
  42.4 1.9 %reshape.35 = bf16[64,2,1536]{2,1,0:T(2,128)(2,1)} reshape(bf16[128,1536]{1,0:T(8,128)(2,1)} %fusion.40) | data formatting | bytes 786432 | tf_op jit(solution)/shard_map/reshape.16
  44.3 2.6 %fusion.12 = f32[64,1,2,768]{3,0,2,1:T(8,128)} fusion(bf16[1,768,1536]{2,1,0:T(8,128)(2,1)S(1)} %copy-done, bf16[64,2,1536]{2,1,0:T(2,128)(2,1)} %reshape.35), kind=kOutput, calls=%fused_computation.17 | convolution fusion | flops 301989888 | bytes 3145728 | tf_op jit(solution)/shard_map/dot_general | solution.py:21
  46.9 0.0 reduce-scatter.6.cloned.1.call-update
  46.9 0.0 reduce-scatter.10.cloned.1.call-start
  47.0 2.3 %fusion.5 = bf16[1,1536,768]{2,1,0:T(8,128)(2,1)} fusion(bf16[128,768]{1,0:T(8,128)(2,1)S(1)} %reshape_squeeze.6, f32[128,1536]{1,0:T(8,128)S(1)} %fusion.8), kind=kOutput, calls=%fused_computation.7 | convolution fusion | flops 304939008 | bytes 3342336 | tf_op jit(solution)/shard_map/dot_general | solution.py:15
  49.3 12.2 %copy.44 = bf16[1,1536,768]{1,0,2:T(2,128)(2,1)} copy(bf16[1,1536,768]{2,1,0:T(8,128)(2,1)} %fusion.5) | data formatting | bytes 4718592
  61.5 4.4 %copy.63 = bf16[768,1,1536]{2,0,1:T(8,128)(2,1)} copy(bf16[768,1,1536]{2,1,0:T(2,128)(2,1)} %bitcast.69) | data formatting | bytes 4718592
  65.9 0.0 reduce-scatter.8.cloned.1.call-start
  65.9 0.9 copy-done.1
  66.8 2.2 %fusion.4 = bf16[1,768,1536]{2,1,0:T(8,128)(2,1)} fusion(bf16[128,768]{1,0:T(8,128)(2,1)S(1)} %reshape_squeeze.7, bf16[128,1536]{1,0:T(8,128)(2,1)S(1)} %copy-done.1), kind=kOutput, calls=%fused_computation.6 | convolution fusion | flops 303169536 | bytes 2949120 | tf_op jit(solution)/shard_map/dot_general | solution.py:18
  69.1 0.0 reduce-scatter.8.cloned.1.call-update
  69.1 0.9 copy-done.8
  70.0 1.8 %fusion.25 = f32[4,196,16]{1,2,0:T(8,128)S(1)} fusion(bf16[4,16,768]{2,1,0:T(8,128)(2,1)S(1)} %copy-done.8, bf16[4,196,768]{2,0,1:T(4,128)(2,1)} %param.11), kind=kOutput, calls=%fused_computation.34 | convolution fusion | flops 19267584 | bytes 1352704 | tf_op jit(solution)/shard_map/bmd,bsd->bms/dot_general | solution.py:73
  71.8 1.0 convert_element_type.44
  72.8 0.7 copy.38
  73.5 3.5 %all-to-all-start.2 = ((bf16[32,1,2,768]{3,2,1,0:T(2,128)(2,1)}), bf16[32,1,2,768]{3,2,1,0:T(2,128)(2,1)S(1)}, u32[]{:S(2)}, u32[]{:S(2)}) async-start(bf16[32,1,2,768]{3,2,1,0:T(2,128)(2,1)} %copy.38), calls=%async_computation.3 | async-start | bytes 196608 | tf_op jit(solution)/shard_map/all_to_all | solution.py:70
  77.1 0.2 fusion.23
  77.3 6.8 %all-to-all-done.2 = bf16[32,1,2,768]{3,2,1,0:T(2,128)(2,1)S(1)} async-done(((bf16[32,1,2,768]{3,2,1,0:T(2,128)(2,1)}), bf16[32,1,2,768]{3,2,1,0:T(2,128)(2,1)S(1)}, u32[]{:S(2)}, u32[]{:S(2)}) %all-to-all-start.2) | async-done | bytes 98336 | tf_op jit(solution)/shard_map/all_to_all | solution.py:70
  84.1 0.1 copy.64
  84.3 1.7 %convolution_bitcast_fusion = f32[4,196,16]{1,2,0:T(8,128)S(1)} fusion(bf16[4,16,768]{2,1,0:T(8,128)(2,1)S(1)} %reshape.36, bf16[4,196,768]{2,0,1:T(4,128)(2,1)} %param.6), kind=kOutput, calls=%fused_computation.24 | convolution fusion | flops 19267584 | bytes 1352704 | tf_op jit(solution)/shard_map/bmd,bsd->bms/dot_general | solution.py:72
  85.9 0.0 copy-start.3
  86.0 2.2 %fusion.28 = f32[4,196,768]{2,1,0:T(8,128)} fusion(f32[4,196,16]{1,2,0:T(8,128)S(1)} %fusion.23, f32[4,196,16]{1,2,0:T(8,128)S(1)} %convolution_bitcast_fusion, bf16[768,16]{0,1:T(8,128)(2,1)S(1)} %copy-done.6, f32[4,196,16]{1,2,0:T(8,128)S(1)} %copy-done.4, f32[4,16]{1,0:T(4,128)S(1)} %get-tuple-element.18), kind=kOutput, calls=%fused_computation.37 | convolution fusion | flops 19355652 | bytes 2583808 | tf_op jit(solution)/shard_map/bms,ds->bmd/dot_general | solution.py:83
  88.1 3.6 %add_convert_fusion = bf16[4,196,768]{2,1,0:T(8,128)(2,1)} fusion(f32[4,196,768]{2,1,0:T(8,128)} %fusion.28, bf16[4,16,768]{2,1,0:T(8,128)(2,1)S(1)} %reshape.36, f32[4,16]{1,0:T(4,128)S(1)} %get-tuple-element.18, f32[4,196,16]{1,2,0:T(8,128)S(1)} %copy-done.3), kind=kOutput, calls=%fused_computation.8 | convolution fusion | flops 20509700 | bytes 3761408 | tf_op jit(solution)/shard_map/bms,bsd->bmd/dot_general | solution.py:81
  91.7 2.8 %copy.43 = bf16[4,196,768]{2,0,1:T(4,128)(2,1)} copy(bf16[4,196,768]{2,1,0:T(8,128)(2,1)} %add_convert_fusion) | data formatting | bytes 2408448
  94.6 1.7 %convolution_bitcast_fusion.1 = f32[768,16]{0,1:T(8,128)S(1)} fusion(f32[4,196,16]{1,2,0:T(8,128)S(1)} %fusion.23, f32[4,196,16]{1,2,0:T(8,128)S(1)} %convolution_bitcast_fusion, bf16[4,196,768]{2,0,1:T(4,128)(2,1)} %param.6, f32[4,196,16]{1,2,0:T(8,128)S(1)} %copy-done.4, f32[4,16]{1,0:T(4,128)S(1)} %get-tuple-element.18), kind=kOutput, calls=%fused_computation.33 | convolution fusion | flops 19355652 | bytes 1404160 | tf_op jit(solution)/shard_map/bmd,bms->ds/dot_general | solution.py:85
  96.3 13.2 %psum.14 = f32[768,16]{0,1:T(8,128)S(1)} all-reduce(f32[768,16]{0,1:T(8,128)S(1)} %convolution_bitcast_fusion.1), channel_id=1, replica_groups=mesh['expert'=8,'pair'=2,'dp'=2] {'pair','dp'}, use_global_device_ids=true, to_apply=%region_7.0 | all-reduce | flops 12288 | bytes 98304 | tf_op jit(solution)/shard_map/psum | solution.py:86
  109.5 35.1 %psum.15 = f32[768,16]{0,1:T(8,128)} all-reduce(f32[768,16]{0,1:T(8,128)S(1)} %psum.14), channel_id=1, replica_groups=mesh['expert'=8,'pair'=2,'dp'=2] {'expert'}, use_global_device_ids=true, to_apply=%region_8.0 | all-reduce | flops 12288 | bytes 98304 | tf_op jit(solution)/shard_map/psum | solution.py:86
  144.6 3.9 %reshape_bitcast_fusion = bf16[1,1536,384]{1,0,2:T(2,128)(2,1)} fusion(bf16[384,1536]{1,0:T(8,128)(2,1)} %reduce-scatter.10.cloned.1.call-done), kind=kLoop, calls=%fused_computation.10 | loop fusion | bytes 2359296
  148.5 6.4 %copy.45 = bf16[1,1536,384]{2,1,0:T(8,128)(2,1)} copy(bf16[1,1536,384]{1,0,2:T(2,128)(2,1)} %reshape_bitcast_fusion) | data formatting | bytes 2359296
  (21 shorter events, 0.2 us)
Async XLA Ops:
  7.2 31.8 %copy-start = (bf16[1,768,1536]{2,1,0:T(8,128)(2,1)S(1)}, bf16[1,768,1536]{2,1,0:T(8,128)(2,1)}, u32[]{:S(2)}) copy-start(bf16[1,768,1536]{2,1,0:T(8,128)(2,1)} %param.8) | copy-start | bytes 7077892
  9.0 12.7 %copy-start.2 = (f32[4,196,16]{1,2,0:T(8,128)}, f32[4,196,16]{1,2,0:T(8,128)S(1)}, u32[]{:S(2)}) copy-start(f32[4,196,16]{1,2,0:T(8,128)S(1)} %fusion.32) | copy-start | bytes 150532
  12.1 14.4 %all-to-all-start = ((bf16[4,8,2,768]{3,2,0,1:T(2,128)(2,1)}), bf16[4,8,2,768]{3,2,0,1:T(2,128)(2,1)S(1)}, u32[]{:S(2)}, u32[]{:S(2)}) async-start(bf16[4,8,2,768]{3,2,0,1:T(2,128)(2,1)} %copy.32), calls=%async_computation | async-start | bytes 196608 | tf_op jit(solution)/shard_map/all_to_all | solution.py:49
  26.5 10.4 %all-to-all-start.1 = ((bf16[4,8,2,768]{3,2,0,1:T(2,128)(2,1)}), bf16[4,8,2,768]{3,2,0,1:T(2,128)(2,1)S(1)}, u32[]{:S(2)}, u32[]{:S(2)}) async-start(bf16[4,8,2,768]{3,2,0,1:T(2,128)(2,1)} %copy.35), calls=%async_computation.1 | async-start | bytes 196608 | tf_op jit(solution)/shard_map/all_to_all | solution.py:48
  29.8 42.0 %reduce-scatter.6.cloned.1.call-start = ((), (), s32[]{:S(2)}) async-start(), calls=%async_computation.6 | async-start | bytes 589824 | tf_op jit(solution)/shard_map/reduce_scatter | solution.py:62
  38.9 1.7 %copy-start.7 = (bf16[1,1536,768]{2,1,0:T(8,128)(2,1)S(1)}, bf16[1,1536,768]{2,1,0:T(8,128)(2,1)}, u32[]{:S(2)}) copy-start(bf16[1,1536,768]{2,1,0:T(8,128)(2,1)} %param.9) | copy-start | bytes 7077892
  46.9 97.7 %reduce-scatter.10.cloned.1.call-start = ((), (), s32[]{:S(2)}) async-start(), calls=%async_computation.8 | async-start | bytes 3538944
  65.8 1.0 copy-start.1
  65.9 89.1 %reduce-scatter.8.cloned.1.call-start = ((), (), s32[]{:S(2)}) async-start(), calls=%async_computation.7 | async-start | bytes 3538944 | tf_op jit(solution)/shard_map/reduce_scatter | solution.py:63
  69.1 0.9 copy-start.8
  70.0 7.1 %copy-start.5 = (f32[4,196,16]{1,2,0:T(8,128)S(1)}, f32[4,196,16]{1,2,0:T(8,128)}, u32[]{:S(2)}) copy-start(f32[4,196,16]{1,2,0:T(8,128)} %get-tuple-element.17) | copy-start | bytes 150532
  73.5 12.4 %copy-start.4 = (f32[4,196,16]{1,2,0:T(8,128)S(1)}, f32[4,196,16]{1,2,0:T(8,128)}, u32[]{:S(2)}) copy-start(f32[4,196,16]{1,2,0:T(8,128)} %get-tuple-element.19) | copy-start | bytes 150532
  73.5 12.4 %copy-start.6 = (bf16[768,16]{0,1:T(8,128)(2,1)S(1)}, bf16[768,16]{0,1:T(8,128)(2,1)}, u32[]{:S(2)}) copy-start(bf16[768,16]{0,1:T(8,128)(2,1)} %param.7) | copy-start | bytes 73732
  73.5 10.6 %all-to-all-start.2 = ((bf16[32,1,2,768]{3,2,1,0:T(2,128)(2,1)}), bf16[32,1,2,768]{3,2,1,0:T(2,128)(2,1)S(1)}, u32[]{:S(2)}, u32[]{:S(2)}) async-start(bf16[32,1,2,768]{3,2,1,0:T(2,128)(2,1)} %copy.38), calls=%async_computation.3 | async-start | bytes 196608 | tf_op jit(solution)/shard_map/all_to_all | solution.py:70
  85.9 2.2 %copy-start.3 = (f32[4,196,16]{1,2,0:T(8,128)S(1)}, f32[4,196,16]{1,2,0:T(8,128)}, u32[]{:S(2)}) copy-start(f32[4,196,16]{1,2,0:T(8,128)} %copy-done.2) | copy-start | bytes 150532
Sparse Core Ops, SparseCore 0:
  47.1 5.4 reduce-scatter.5
  66.0 32.4 reduce-scatter.9
  101.3 34.9 reduce-scatter.7
